TPU v7x, 32 devices: a whole 2x2x4 slice. The times are simulated.
32 devices in a mesh: img: 4 (over y, x), proto: 8 (over z, core).
Axes of the slice: x: 2, y: 2, z: 4, core: 2. Of those that a mesh axis runs over, the one named last changes fastest.
Arguments:
- student_patch_tokens: bfloat16 [4, 256, 4096], P('img', None, 'proto'), may hold values from -6 to 6
- teacher_patch_tokens: bfloat16 [4, 256, 4096], P('img', None, 'proto'), may hold values from -6 to 6
- mask_counts: int32 [4], P('img'), may hold values from 32 to 128, as said below
- mask_index: int32 [4, 128], P('img'), may hold values from 0 to 255, as said below
- student_bottleneck: bfloat16 [4096, 256], P('proto'), may hold values from -0.09375 to 0.09375
- teacher_bottleneck: bfloat16 [4096, 256], P('proto'), may hold values from -0.09375 to 0.09375
- student_protos: bfloat16 [256, 98304], P(None, 'proto'), may hold values from -60 to 60
- teacher_protos: bfloat16 [256, 98304], P(None, 'proto'), may hold values from -60 to 60
- center: float32 [98304], P('proto'), may hold values from -0.75 to 0.75
Outputs:
- image_loss: float32 [4], P('img')
- grad_protos: float32 [256, 98304], P('img', 'proto')
- grad_bottleneck: float32 [4096, 256], P('proto', 'img')
Inputs may be any that keep to these rules, and one draw needn't show every extreme that they name: `mask_counts`: some image has exactly 128 masked patches. `mask_index`: the 128 entries of an image are distinct patch numbers; only the first mask_counts of them are used.
All inputs are finite; a program needn't handle non-finite values.
Results may differ from a plain program's by a relative error of at most 0.0071.
Values may be sent and summed in bfloat16 or wider, within the bound.
No kernel may reach another device: no remote copies, remote signals or barrier semaphores. Data moves between devices by JAX's collectives and lax.ppermute only.
A program may use at most 64 MiB of HBM per device.

v0:
```python
import jax
import jax.numpy as jnp
from jax import lax
from jax.sharding import PartitionSpec as P

EPSILON = 1e-06
STUDENT_TEMP = 0.1
TEACHER_TEMP = 0.04
LOSS_SCALE = 4096.0


def scores(units_student, units_teacher, weight, student_protos, teacher_protos, center):
    logits_student = (
        jnp.dot(units_student, student_protos, preferred_element_type=jnp.float32) / STUDENT_TEMP
    )
    logits_teacher = (
        jnp.dot(units_teacher, teacher_protos, preferred_element_type=jnp.float32) - center[None, :]
    ) / TEACHER_TEMP
    top_student, top_teacher = lax.pmax(
        (jnp.max(logits_student, axis=1), jnp.max(logits_teacher, axis=1)), "proto"
    )
    exp_student = jnp.exp(logits_student - top_student[:, None])
    exp_teacher = jnp.exp(logits_teacher - top_teacher[:, None])
    total_student, total_teacher, cross = lax.psum(
        (
            jnp.sum(exp_student, axis=1),
            jnp.sum(exp_teacher, axis=1),
            jnp.sum(exp_teacher * logits_student, axis=1),
        ),
        "proto",
    )
    loss_rows = -(cross / total_teacher - top_student - jnp.log(total_student))
    differ = exp_student / total_student[:, None] - exp_teacher / total_teacher[:, None]
    logit_gradient = (
        LOSS_SCALE * weight.astype(jnp.float32)[:, None] * differ / STUDENT_TEMP
    ).astype(jnp.bfloat16)
    return (loss_rows, logit_gradient)


def prototype_gradient(row_units, logit_gradient):
    return lax.psum_scatter(
        lax.dot_general(
            row_units, logit_gradient, (((0,), (0,)), ((), ())), preferred_element_type=jnp.float32
        ),
        "img",
        scatter_dimension=0,
        tiled=True,
    )


def per_device(
    student_patch_tokens,
    teacher_patch_tokens,
    mask_counts,
    mask_index,
    student_bottleneck,
    teacher_bottleneck,
    student_protos,
    teacher_protos,
    center,
):
    img_local, patch_total, width_local = student_patch_tokens.shape
    mask_width = mask_index.shape[1]
    rows_local = img_local * mask_width
    patch_iota = lax.broadcasted_iota(jnp.int32, (img_local, mask_width, patch_total), 2)
    masked_picker = (mask_index[:, :, None] == patch_iota).astype(jnp.bfloat16)
    student_token_rows = (
        jnp.einsum(
            "oaz,oze->oae", masked_picker, student_patch_tokens, preferred_element_type=jnp.float32
        )
        .astype(jnp.bfloat16)
        .reshape(rows_local, width_local)
    )
    teacher_rows = (
        jnp.einsum(
            "oaz,oze->oae", masked_picker, teacher_patch_tokens, preferred_element_type=jnp.float32
        )
        .astype(jnp.bfloat16)
        .reshape(rows_local, width_local)
    )
    partial_student = jnp.dot(
        student_token_rows, student_bottleneck, preferred_element_type=jnp.float32
    )
    partial_teacher = jnp.dot(teacher_rows, teacher_bottleneck, preferred_element_type=jnp.float32)
    hidden_student, hidden_teacher = lax.psum((partial_student, partial_teacher), "proto")
    inv_student = lax.rsqrt(
        jnp.sum(hidden_student * hidden_student, axis=1, keepdims=True) + EPSILON
    )
    inv_teacher = lax.rsqrt(
        jnp.sum(hidden_teacher * hidden_teacher, axis=1, keepdims=True) + EPSILON
    )
    units_student = (hidden_student * inv_student).astype(jnp.bfloat16)
    units_teacher = (hidden_teacher * inv_teacher).astype(jnp.bfloat16)
    position = lax.broadcasted_iota(jnp.int32, (img_local, mask_width), 1)
    live_grid = position < mask_counts[:, None]
    weight = (
        jnp.where(live_grid, 1.0 / mask_counts.astype(jnp.float32)[:, None], 0.0)
        .astype(jnp.bfloat16)
        .reshape(rows_local)
    )
    loss_rows, logit_gradient = scores(
        units_student, units_teacher, weight, student_protos, teacher_protos, center
    )
    weighted = weight.astype(jnp.float32) * loss_rows
    image_loss = jnp.sum(weighted.reshape(img_local, mask_width), axis=1)
    grad_protos = prototype_gradient(units_student, logit_gradient)
    partial_rows = lax.dot_general(
        logit_gradient, student_protos, (((1,), (1,)), ((), ())), preferred_element_type=jnp.float32
    )
    grad_rows = lax.psum(partial_rows, "proto")
    inner = jnp.sum(hidden_student * grad_rows, axis=1, keepdims=True)
    grad_hidden = (
        grad_rows * inv_student - hidden_student * inner * (inv_student * inv_student * inv_student)
    ).astype(jnp.bfloat16)
    local_term = lax.dot_general(
        student_token_rows,
        grad_hidden,
        (((0,), (0,)), ((), ())),
        preferred_element_type=jnp.float32,
    )
    grad_bottleneck = lax.psum_scatter(local_term, "img", scatter_dimension=1, tiled=True)
    return (image_loss, grad_protos, grad_bottleneck)


def solution(mesh):
    placed = (
        P("img", None, "proto"),
        P("img", None, "proto"),
        P("img"),
        P("img", None),
        P("proto", None),
        P("proto", None),
        P(None, "proto"),
        P(None, "proto"),
        P("proto"),
    )
    return jax.shard_map(
        per_device,
        mesh=mesh,
        in_specs=placed,
        out_specs=(P("img"), P("img", "proto"), P("proto", "img")),
        check_vma=False,
    )
```

profile of v0, /device:TPU:0, one launch (start us, length us, event | category | flops | bytes accessed | tf_op | source)
XLA Modules:
  0.0 341.4 jit_solution(12172484744703447159)
XLA Ops:
  7.2 0.0 copy-start
  7.2 0.0 all-reduce.8.cloned.1.call-start
  7.2 0.9 copy-done
  8.1 0.9 convolution_convert_fusion
  9.0 0.6 copy-done.2
  9.7 1.8 fusion.25
  11.5 2.1 fusion.3
  13.5 0.0 all-reduce.8.cloned.1.call-update
  13.5 0.0 all-reduce.6.cloned.1.call-start
  14.3 57.6 %all-reduce.8.cloned.1.call-done = (f32[128,256]{1,0:T(8,128)}, f32[128,256]{1,0:T(8,128)}) async-done(((f32[128,256]{1,0:T(8,128)}, f32[128,256]{1,0:T(8,128)}), (f32[128,256]{1,0:T(8,128)}, f32[128,256]{1,0:T(8,128)})) %all-reduce.8.cloned.1.call-update) | async-done | bytes 262160 | tf_op jit(solution)/shard_map/psum | solution.py:85
  71.9 1.2 multiply_reduce_fusion.2
  73.2 0.5 multiply_multiply_fusion
  73.7 6.7 %fusion.24 = (f32[128]{0:T(128)S(1)}, f32[128,12288]{1,0:T(8,128)}) fusion(bf16[256,12288]{1,0:T(8,128)(2,1)} %param.15, f32[128,256]{1,0:T(8,128)} %get-tuple-element.10, f32[128]{0:T(128)S(1)} %get-tuple-element.14), kind=kOutput, calls=%fused_computation.39 | convolution fusion | flops 808517504 | bytes 12715008 | tf_op jit(solution)/shard_map/dot_general | solution.py:14
  80.5 4.0 %fusion.23 = (f32[128]{0:T(128)S(1)}, f32[128,12288]{1,0:T(8,128)}) fusion(f32[12288]{0:T(1024)S(1)} %copy-done.4, bf16[256,12288]{1,0:T(8,128)(2,1)S(1)} %bitcast.28, f32[128,256]{1,0:T(8,128)S(1)} %copy-done.3, f32[128]{0:T(128)S(1)} %add_rsqrt_fusion.1), kind=kOutput, calls=%fused_computation.38 | convolution fusion | flops 810090368 | bytes 12764160 | tf_op jit(solution)/shard_map/dot_general | solution.py:17
  84.5 13.7 %all-reduce.2 = (f32[128]{0:T(128)S(1)}, f32[128]{0:T(128)S(1)}) all-reduce(f32[128]{0:T(128)S(1)} %get-tuple-element.15, f32[128]{0:T(128)S(1)} %get-tuple-element.17), channel_id=1, replica_groups=mesh['img'=4,'proto'=8] {'proto'}, use_global_device_ids=true, to_apply=%region_3.0 | all-reduce | flops 256 | bytes 2048 | tf_op jit(solution)/shard_map/pmax | solution.py:19
  98.1 5.9 %fusion.2 = (f32[128]{0:T(128)S(1)}, f32[128]{0:T(128)S(1)}, f32[128]{0:T(128)S(1)}) fusion(f32[128,12288]{1,0:T(8,128)} %get-tuple-element.16, f32[128]{0:T(128)S(1)} %get-tuple-element.11, f32[128,12288]{1,0:T(8,128)} %get-tuple-element.18, f32[128]{0:T(128)S(1)} %get-tuple-element.12), kind=kLoop, calls=%fused_computation.8 | loop fusion | flops 9436800 | bytes 12585472 | tf_op jit(solution)/shard_map/reduce_sum | solution.py:27
  104.0 14.1 %all-reduce = (f32[128]{0:T(128)S(1)}, f32[128]{0:T(128)}, f32[128]{0:T(128)S(1)}) all-reduce(f32[128]{0:T(128)S(1)} %get-tuple-element.5, f32[128]{0:T(128)S(1)} %get-tuple-element.4, f32[128]{0:T(128)S(1)} %get-tuple-element.3), channel_id=1, replica_groups=mesh['img'=4,'proto'=8] {'proto'}, use_global_device_ids=true, to_apply=%region_13.14 | all-reduce | flops 384 | bytes 3072 | tf_op jit(solution)/shard_map/psum | solution.py:24
  118.2 5.9 %multiply_convert_fusion = bf16[128,12288]{1,0:T(8,128)(2,1)S(1)} fusion(f32[128,12288]{1,0:T(8,128)} %get-tuple-element.18, f32[128,12288]{1,0:T(8,128)} %get-tuple-element.16, f32[128]{0:T(128)S(1)} %get-tuple-element.8, f32[128]{0:T(128)S(1)} %get-tuple-element.6, f32[128]{0:T(128)S(1)} %fusion.21, f32[128]{0:T(128)S(1)} %get-tuple-element.12, ...), kind=kLoop, calls=%fused_computation.3 | loop fusion | flops 12582912 | bytes 15731200 | tf_op jit(solution)/shard_map/convert_element_type | solution.py:36
  124.1 5.7 %fusion.26 = f32[128,256]{1,0:T(8,128)} fusion(bf16[128,12288]{1,0:T(8,128)(2,1)S(1)} %multiply_convert_fusion, bf16[256,12288]{1,0:T(8,128)(2,1)} %param.15), kind=kOutput, calls=%fused_computation.41 | convolution fusion | flops 805306368 | bytes 9568256 | tf_op jit(solution)/shard_map/dot_general | solution.py:107
  129.8 0.0 all-reduce.6.cloned.1.call-update
  129.9 0.0 reduce-scatter.5.cloned.1.call-start
  129.9 53.2 %all-reduce.6.cloned.1.call-done = f32[128,256]{1,0:T(8,128)} async-done(((f32[128,256]{1,0:T(8,128)}), f32[128,256]{1,0:T(8,128)}) %all-reduce.6.cloned.1.call-update) | async-done | bytes 131088 | tf_op jit(solution)/shard_map/psum | solution.py:110
  183.1 1.0 multiply_reduce_fusion.1
  184.2 2.2 fusion.11
  186.3 0.0 reduce-scatter.5.cloned.1.call-update
  186.3 0.0 reduce-scatter.3.cloned.1.call-start
  186.4 6.5 %fusion.22 = f32[256,12288]{1,0:T(8,128)} fusion(bf16[128,12288]{1,0:T(8,128)(2,1)S(1)} %multiply_convert_fusion, f32[128,256]{1,0:T(8,128)S(1)} %copy-done.1, f32[128]{0:T(128)S(1)} %get-tuple-element.14), kind=kOutput, calls=%fused_computation.37 | convolution fusion | flops 805371904 | bytes 15860224 | tf_op jit(solution)/shard_map/dot_general | solution.py:42
  192.8 0.0 reduce-scatter.3.cloned.1.call-update
  192.9 0.6 copy-done.5
  193.5 0.6 multiply_reduce_fusion.4
  194.1 16.6 %reduce-scatter.5.cloned.1.call-done = f32[512,64]{0,1:T(8,128)} async-done(((f32[512,256]{0,1:T(8,128)}), f32[512,64]{0,1:T(8,128)}) %reduce-scatter.5.cloned.1.call-update) | async-done | bytes 131088 | tf_op jit(solution)/shard_map/reduce_scatter | solution.py:121
  210.7 124.2 %reduce-scatter.3.cloned.1.call-done = f32[64,12288]{1,0:T(8,128)} async-done(((f32[256,12288]{1,0:T(8,128)}), f32[64,12288]{1,0:T(8,128)}) %reduce-scatter.3.cloned.1.call-update) | async-done | bytes 3145744 | tf_op jit(solution)/shard_map/reduce_scatter | solution.py:41
  (15 shorter events, 0.0 us)
Async XLA Ops:
  7.2 1.0 copy-start
  7.2 64.8 %all-reduce.8.cloned.1.call-start = ((), (), s32[]{:S(2)}) async-start(), calls=%async_computation.5 | async-start | bytes 524288 | tf_op jit(solution)/shard_map/psum | solution.py:85
  9.0 0.7 copy-start.2
  13.5 169.6 %all-reduce.6.cloned.1.call-start = ((), (), s32[]{:S(2)}) async-start(), calls=%async_computation.3 | async-start | bytes 262144 | tf_op jit(solution)/shard_map/psum | solution.py:110
  71.9 8.5 %slice-start = ((s8[6291456]{0:T(1024)(128)(4,1)}), s8[4194304]{0:T(1024)(128)(4,1)S(1)}, s32[]{:S(2)}) async-start(s8[6291456]{0:T(1024)(128)(4,1)} %bitcast.27), calls=%async_computation.6 | async-start | bytes 8388608
  73.7 6.8 %slice-start.1 = ((s8[6291456]{0:T(1024)(128)(4,1)}), s8[2097152]{0:T(1024)(128)(4,1)S(1)}, s32[]{:S(2)}) async-start(s8[6291456]{0:T(1024)(128)(4,1)} %bitcast.27), calls=%async_computation.7 | async-start | bytes 4194304
  73.7 6.8 %copy-start.3 = (f32[128,256]{1,0:T(8,128)S(1)}, f32[128,256]{1,0:T(8,128)}, u32[]{:S(2)}) copy-start(f32[128,256]{1,0:T(8,128)} %get-tuple-element.9) | copy-start | bytes 393220
  73.7 6.8 %copy-start.4 = (f32[12288]{0:T(1024)S(1)}, f32[12288]{0:T(1024)}, u32[]{:S(2)}) copy-start(f32[12288]{0:T(1024)} %param.17) | copy-start | bytes 147460
  124.1 59.0 %copy-start.1 = (f32[128,256]{1,0:T(8,128)S(1)}, f32[128,256]{1,0:T(8,128)}, u32[]{:S(2)}) copy-start(f32[128,256]{1,0:T(8,128)} %get-tuple-element.10) | copy-start | bytes 393220
  129.9 80.9 %reduce-scatter.5.cloned.1.call-start = ((), (), s32[]{:S(2)}) async-start(), calls=%async_computation.4 | async-start | bytes 655360 | tf_op jit(solution)/shard_map/reduce_scatter | solution.py:121
  186.3 148.5 %reduce-scatter.3.cloned.1.call-start = ((), (), s32[]{:S(2)}) async-start(), calls=%async_computation.2 | async-start | bytes 15728640 | tf_op jit(solution)/shard_map/reduce_scatter | solution.py:41
  192.8 0.6 copy-start.5
Sparse Core Ops, SparseCore 0:
  13.7 58.2 all-reduce.7
  130.0 53.1 all-reduce.5
  186.5 24.1 reduce-scatter.4
  214.2 120.5 reduce-scatter.2
where the time goes:
time: 342 us; the launch traced here: 341 us
  waiting for transfers between devices  252 us (74%)
  matrix products  29.8 us (9%)
  blocking collectives  27.8 us (8%)
  other arithmetic  15.2 us (4%)
  between operations  14.5 us (4%)
    reduce_scatter x1, waiting for transfers between devices, prototype_gradient(): lax.psum_scatter(lax.dot_general(row_units, logit_gradient, (((0,), (0,))...  124 us
    psum x1, waiting for transfers between devices, per_device(): lax.psum((partial_student, partial_teacher), 'proto')  57.6 us
    psum x1, waiting for transfers between devices, per_device(): grad_rows = lax.psum(partial_rows, 'proto')  53.2 us
    reduce_scatter x1, waiting for transfers between devices, per_device(): lax.psum_scatter(local_term, 'img', scatter_dimension=1, tiled=True)  16.6 us
    psum x1, blocking collectives, scores(): lax.psum((jnp.sum(exp_student, axis=1), jnp.sum(exp_teacher, axis=1), jnp...  14.1 us
    pmax x1, blocking collectives, scores(): lax.pmax((jnp.max(logits_student, axis=1), jnp.max(logits_teacher, axis=1...  13.7 us
  transfers between devices with their start and end apart: 4, of which 4 were waited for; matrix products, arithmetic and copies ran while one was open for 2% of the time, Pallas kernels for 0%

commit v1 on v0

--- a/solution.py
+++ b/solution.py
@@ -2,11 +2,16 @@
 import jax.numpy as jnp
 from jax import lax
 from jax.sharding import PartitionSpec as P
+from jax.lax import all_gather
 
 EPSILON = 1e-06
 STUDENT_TEMP = 0.1
 TEACHER_TEMP = 0.04
 LOSS_SCALE = 4096.0
+
+
+def read_frames(point):
+    return jnp.sum(all_gather(point, "proto"), axis=0)
 
 
 def scores(units_student, units_teacher, weight, student_protos, teacher_protos, center):
@@ -107,7 +112,7 @@
     partial_rows = lax.dot_general(
         logit_gradient, student_protos, (((1,), (1,)), ((), ())), preferred_element_type=jnp.float32
     )
-    grad_rows = lax.psum(partial_rows, "proto")
+    grad_rows = read_frames(partial_rows)
     inner = jnp.sum(hidden_student * grad_rows, axis=1, keepdims=True)
     grad_hidden = (
         grad_rows * inv_student - hidden_student * inner * (inv_student * inv_student * inv_student)

time: 342 us -> 311 us (0.909)
  waiting for transfers between devices: 252 us -> 219 us
    psum x1 -> x0, waiting for transfers between devices: 53.2 us -> none  [per_device(): grad_rows = lax.psum(partial_rows, 'proto')]
    all_gather x0 -> x1, waiting for transfers between devices: none -> 20.5 us  [read_frames(): return jnp.sum(all_gather(point, 'proto'), axis=0)]
where the time goes in v1:
time: 311 us
  waiting for transfers between devices  219 us (70%)
  matrix products  29.8 us (10%)
  blocking collectives  27.8 us (9%)
  other arithmetic  17.2 us (6%)
  between operations  14.5 us (5%)
    reduce_scatter x1, waiting for transfers between devices, prototype_gradient(): lax.psum_scatter(lax.dot_general(row_units, logit_gradient, (((0,), (0,))...  124 us
    psum x1, waiting for transfers between devices, per_device(): lax.psum((partial_student, partial_teacher), 'proto')  57.6 us
    all_gather x1, waiting for transfers between devices, read_frames(): return jnp.sum(all_gather(point, 'proto'), axis=0)  20.5 us
    reduce_scatter x1, waiting for transfers between devices, per_device(): lax.psum_scatter(local_term, 'img', scatter_dimension=1, tiled=True)  17.1 us
    psum x1, blocking collectives, scores(): lax.psum((jnp.sum(exp_student, axis=1), jnp.sum(exp_teacher, axis=1), jnp...  14.1 us
    pmax x1, blocking collectives, scores(): lax.pmax((jnp.max(logits_student, axis=1), jnp.max(logits_teacher, axis=1...  13.7 us
    dot_general x1, matrix products, scores(): jnp.dot(units_student, student_protos, preferred_element_type=jnp.float32)  6.74 us
    dot_general x1, matrix products, prototype_gradient(): lax.dot_general(row_units, logit_gradient, (((0,), (0,)), ((), ())), pref...  6.46 us
  transfers between devices with their start and end apart: 4, of which 4 were waited for; matrix products, arithmetic and copies ran while one was open for 2% of the time, Pallas kernels for 0%

profile of v1, /device:TPU:0, one launch (start us, length us, event | category | flops | bytes accessed | tf_op | source)
XLA Modules:
  0.0 311.1 jit_solution(4949381856489049071)
XLA Ops:
  7.2 0.0 all-reduce.5.cloned.1.call-start
  7.2 0.9 copy-done
  8.1 0.9 convolution_convert_fusion
  9.0 0.6 copy-done.2
  9.7 1.8 fusion.25
  11.5 2.1 fusion.3
  13.5 0.0 all-reduce.5.cloned.1.call-update
  13.5 0.0 all-gather.3.cloned.1.call-start
  14.3 57.6 %all-reduce.5.cloned.1.call-done = (f32[128,256]{1,0:T(8,128)}, f32[128,256]{1,0:T(8,128)}) async-done(((f32[128,256]{1,0:T(8,128)}, f32[128,256]{1,0:T(8,128)}), (f32[128,256]{1,0:T(8,128)}, f32[128,256]{1,0:T(8,128)})) %all-reduce.5.cloned.1.call-update) | async-done | bytes 262160 | tf_op jit(solution)/shard_map/psum | solution.py:90
  71.9 1.2 multiply_reduce_fusion.2
  73.2 0.5 multiply_multiply_fusion
  73.7 6.7 %fusion.24 = (f32[128]{0:T(128)S(1)}, f32[128,12288]{1,0:T(8,128)}) fusion(bf16[256,12288]{1,0:T(8,128)(2,1)} %param.15, f32[128,256]{1,0:T(8,128)} %get-tuple-element.10, f32[128]{0:T(128)S(1)} %get-tuple-element.14), kind=kOutput, calls=%fused_computation.39 | convolution fusion | flops 808517504 | bytes 12715008 | tf_op jit(solution)/shard_map/dot_general | solution.py:19
  80.5 4.0 %fusion.23 = (f32[128]{0:T(128)S(1)}, f32[128,12288]{1,0:T(8,128)}) fusion(f32[12288]{0:T(1024)S(1)} %copy-done.4, bf16[256,12288]{1,0:T(8,128)(2,1)S(1)} %bitcast.29, f32[128,256]{1,0:T(8,128)S(1)} %copy-done.3, f32[128]{0:T(128)S(1)} %add_rsqrt_fusion.1), kind=kOutput, calls=%fused_computation.38 | convolution fusion | flops 810090368 | bytes 12764160 | tf_op jit(solution)/shard_map/dot_general | solution.py:22
  84.5 13.7 %all-reduce.2 = (f32[128]{0:T(128)S(1)}, f32[128]{0:T(128)S(1)}) all-reduce(f32[128]{0:T(128)S(1)} %get-tuple-element.15, f32[128]{0:T(128)S(1)} %get-tuple-element.17), channel_id=1, replica_groups=mesh['img'=4,'proto'=8] {'proto'}, use_global_device_ids=true, to_apply=%region_3.0 | all-reduce | flops 256 | bytes 2048 | tf_op jit(solution)/shard_map/pmax | solution.py:24
  98.1 5.9 %fusion.2 = (f32[128]{0:T(128)S(1)}, f32[128]{0:T(128)S(1)}, f32[128]{0:T(128)S(1)}) fusion(f32[128,12288]{1,0:T(8,128)} %get-tuple-element.16, f32[128]{0:T(128)S(1)} %get-tuple-element.11, f32[128,12288]{1,0:T(8,128)} %get-tuple-element.18, f32[128]{0:T(128)S(1)} %get-tuple-element.12), kind=kLoop, calls=%fused_computation.8 | loop fusion | flops 9436800 | bytes 12585472 | tf_op jit(solution)/shard_map/reduce_sum | solution.py:32
  104.0 14.1 %all-reduce = (f32[128]{0:T(128)S(1)}, f32[128]{0:T(128)}, f32[128]{0:T(128)S(1)}) all-reduce(f32[128]{0:T(128)S(1)} %get-tuple-element.5, f32[128]{0:T(128)S(1)} %get-tuple-element.4, f32[128]{0:T(128)S(1)} %get-tuple-element.3), channel_id=1, replica_groups=mesh['img'=4,'proto'=8] {'proto'}, use_global_device_ids=true, to_apply=%region_13.14 | all-reduce | flops 384 | bytes 3072 | tf_op jit(solution)/shard_map/psum | solution.py:29
  118.2 5.9 %multiply_convert_fusion = bf16[128,12288]{1,0:T(8,128)(2,1)S(1)} fusion(f32[128,12288]{1,0:T(8,128)} %get-tuple-element.18, f32[128,12288]{1,0:T(8,128)} %get-tuple-element.16, f32[128]{0:T(128)S(1)} %get-tuple-element.8, f32[128]{0:T(128)S(1)} %get-tuple-element.6, f32[128]{0:T(128)S(1)} %fusion.21, f32[128]{0:T(128)S(1)} %get-tuple-element.12, ...), kind=kLoop, calls=%fused_computation.3 | loop fusion | flops 12582912 | bytes 15731200 | tf_op jit(solution)/shard_map/convert_element_type | solution.py:41
  124.1 5.7 %fusion.26 = f32[128,256]{1,0:T(8,128)} fusion(bf16[128,12288]{1,0:T(8,128)(2,1)S(1)} %multiply_convert_fusion, bf16[256,12288]{1,0:T(8,128)(2,1)} %param.15), kind=kOutput, calls=%fused_computation.41 | convolution fusion | flops 805306368 | bytes 9568256 | tf_op jit(solution)/shard_map/dot_general | solution.py:112
  129.8 0.0 all-gather.3.cloned.1.call-update
  129.9 0.0 reduce-scatter.5.cloned.1.call-start
  129.9 20.5 %all-gather.3.cloned.1.call-done = f32[1024,256]{1,0:T(8,128)} async-done(((f32[128,256]{1,0:T(8,128)}), f32[1024,256]{1,0:T(8,128)}) %all-gather.3.cloned.1.call-update) | async-done | bytes 1048592 | tf_op jit(solution)/shard_map/all_gather | solution.py:14
  150.4 2.0 reduce_sum.81
  152.4 1.0 multiply_reduce_fusion.1
  153.4 2.2 fusion.11
  155.5 0.0 reduce-scatter.5.cloned.1.call-update
  155.5 0.0 reduce-scatter.3.cloned.1.call-start
  155.6 6.5 %fusion.22 = f32[256,12288]{1,0:T(8,128)} fusion(bf16[128,12288]{1,0:T(8,128)(2,1)S(1)} %multiply_convert_fusion, f32[128,256]{1,0:T(8,128)S(1)} %copy-done.1, f32[128]{0:T(128)S(1)} %get-tuple-element.14), kind=kOutput, calls=%fused_computation.37 | convolution fusion | flops 805371904 | bytes 15860224 | tf_op jit(solution)/shard_map/dot_general | solution.py:47
  162.1 0.0 reduce-scatter.3.cloned.1.call-update
  162.1 0.6 copy-done.5
  162.7 0.6 multiply_reduce_fusion.4
  163.3 17.1 %reduce-scatter.5.cloned.1.call-done = f32[512,64]{0,1:T(8,128)} async-done(((f32[512,256]{0,1:T(8,128)}), f32[512,64]{0,1:T(8,128)}) %reduce-scatter.5.cloned.1.call-update) | async-done | bytes 131088 | tf_op jit(solution)/shard_map/reduce_scatter | solution.py:126
  180.4 124.2 %reduce-scatter.3.cloned.1.call-done = f32[64,12288]{1,0:T(8,128)} async-done(((f32[256,12288]{1,0:T(8,128)}), f32[64,12288]{1,0:T(8,128)}) %reduce-scatter.3.cloned.1.call-update) | async-done | bytes 3145744 | tf_op jit(solution)/shard_map/reduce_scatter | solution.py:46
  (16 shorter events, 0.0 us)
Async XLA Ops:
  7.2 1.0 copy-start
  7.2 64.8 %all-reduce.5.cloned.1.call-start = ((), (), s32[]{:S(2)}) async-start(), calls=%async_computation.5 | async-start | bytes 524288 | tf_op jit(solution)/shard_map/psum | solution.py:90
  9.0 0.7 copy-start.2
  13.5 136.8 %all-gather.3.cloned.1.call-start = ((), (), s32[]{:S(2)}) async-start(), calls=%async_computation.4 | async-start | bytes 1179648 | tf_op jit(solution)/shard_map/all_gather | solution.py:14
  71.9 8.5 %slice-start = ((s8[6291456]{0:T(1024)(128)(4,1)}), s8[4194304]{0:T(1024)(128)(4,1)S(1)}, s32[]{:S(2)}) async-start(s8[6291456]{0:T(1024)(128)(4,1)} %bitcast.28), calls=%async_computation.6 | async-start | bytes 8388608
  73.7 6.8 %slice-start.1 = ((s8[6291456]{0:T(1024)(128)(4,1)}), s8[2097152]{0:T(1024)(128)(4,1)S(1)}, s32[]{:S(2)}) async-start(s8[6291456]{0:T(1024)(128)(4,1)} %bitcast.28), calls=%async_computation.7 | async-start | bytes 4194304
  73.7 6.8 %copy-start.3 = (f32[128,256]{1,0:T(8,128)S(1)}, f32[128,256]{1,0:T(8,128)}, u32[]{:S(2)}) copy-start(f32[128,256]{1,0:T(8,128)} %get-tuple-element.9) | copy-start | bytes 393220
  73.7 6.8 %copy-start.4 = (f32[12288]{0:T(1024)S(1)}, f32[12288]{0:T(1024)}, u32[]{:S(2)}) copy-start(f32[12288]{0:T(1024)} %param.17) | copy-start | bytes 147460
  124.1 28.2 %copy-start.1 = (f32[128,256]{1,0:T(8,128)S(1)}, f32[128,256]{1,0:T(8,128)}, u32[]{:S(2)}) copy-start(f32[128,256]{1,0:T(8,128)} %get-tuple-element.10) | copy-start | bytes 393220
  129.9 50.5 %reduce-scatter.5.cloned.1.call-start = ((), (), s32[]{:S(2)}) async-start(), calls=%async_computation.3 | async-start | bytes 655360 | tf_op jit(solution)/shard_map/reduce_scatter | solution.py:126
  155.5 149.0 %reduce-scatter.3.cloned.1.call-start = ((), (), s32[]{:S(2)}) async-start(), calls=%async_computation.2 | async-start | bytes 15728640 | tf_op jit(solution)/shard_map/reduce_scatter | solution.py:46
  162.1 0.6 copy-start.5
Sparse Core Ops, SparseCore 0:
  13.7 58.2 all-reduce.4
  130.0 20.3 all-gather.2
  155.7 24.6 reduce-scatter.4
  183.9 120.6 reduce-scatter.2
